TPU v7x, 32 devices: a whole 2x2x4 slice. The times are simulated.
32 devices in a mesh: slab: 8 (over z, x), pencil: 4 (over y, core).
Axes of the slice: x: 2, y: 2, z: 4, core: 2. Of those that a mesh axis runs over, the one named last changes fastest.
Arguments:
- atom_cell: int32 [3, 262144], P(None, ('slab', 'pencil')), may hold values from 0 to 511, as said below
- charge: float32 [262144], P(('slab', 'pencil')), may hold values from -4 to 4
Outputs:
- potential: float32 [64, 128, 512], P('slab', 'pencil')
- forces: float32 [3, 262144], P(None, ('slab', 'pencil'))
Inputs may be any that keep to these rules, and one draw needn't show every extreme that they name: `atom_cell`: the atoms of rows b * 8192 to (b + 1) * 8192 - 1, with b = s * 4 + r, lie in z planes s * 8 to (s + 1) * 8 - 1 and y rows r * 32 to (r + 1) * 32 - 1. Row 0 is at cell (0, 0, 0) and the last row at cell (63, 127, 511).
All inputs are finite; a program needn't handle non-finite values.
Results may differ from a plain program's by a relative error of at most 0.0003.
Values sent between devices are 32-bit elements; how exact they have to be, the bound alone decides.
A program may use at most 128 MiB of HBM per device.

v0:
```python
from functools import partial
import math
import jax
import jax.numpy as jnp
from jax import lax
from jax.sharding import PartitionSpec as P

CZ = 8
CY = 32
NX = 512
LEVELS = 5
RADIUS = 2
F = 32


def extended(cells, sides, width):
    for axis, dim in sides:
        count = lax.axis_size(axis)
        ends = count - 1
        head = lax.slice_in_dim(cells, 0, width, axis=dim)
        tail = lax.slice_in_dim(cells, cells.shape[dim] - width, cells.shape[dim], axis=dim)
        cells = jnp.concatenate(
            [
                lax.ppermute(tail, axis, [(i, (i + 1) % count) for i in range(ends)]),
                cells,
                lax.ppermute(head, axis, [((i + 1) % count, i) for i in range(ends)]),
            ],
            axis=dim,
        )
    return cells


def kernel_weight(step_z, step_y, step_x):
    squared = step_z * step_z + step_y * step_y + step_x * step_x
    return 1.0 / math.sqrt(squared + 0.25) - 1.0 / math.sqrt(squared + 4.0)


def level_weight(scale, step_z, step_y, step_x):
    squared = step_z * step_z + step_y * step_y + step_x * step_x
    return scale * (1.0 / math.sqrt(squared + 1.0) - 1.0 / math.sqrt(squared + 4.0))


def short_field(padded, plane_count, row_count, row_length, radius_cells, weight_of):
    accumulated = jnp.zeros((plane_count, row_count, row_length), jnp.float32)
    for step_z in range(-radius_cells, radius_cells + 1):
        for step_y in range(-radius_cells, radius_cells + 1):
            for step_x in range(-radius_cells, radius_cells + 1):
                corner_z = radius_cells + step_z
                corner_y = radius_cells + step_y
                corner_x = radius_cells + step_x
                accumulated = (
                    accumulated
                    + weight_of(step_z, step_y, step_x)
                    * padded[
                        corner_z : corner_z + plane_count,
                        corner_y : corner_y + row_count,
                        corner_x : corner_x + row_length,
                    ]
                )
    return accumulated


def restrict(grid):
    planes, rows, length = grid.shape
    return grid.reshape(planes // 2, 2, rows // 2, 2, length // 2, 2).sum(axis=(1, 3, 5))


def restrict_plane(plane):
    rows, length = plane.shape
    return plane.reshape(rows // 2, 2, length // 2, 2).sum(axis=(1, 3))


def interp_matrix(fine_ids, level_count, factor, first_col, width):
    numerator = jnp.clip(2 * fine_ids + 1 - factor, 0, 2 * factor * (level_count - 1))
    lower_index = jnp.minimum(numerator // (2 * factor), level_count - 2)
    fraction = (numerator - lower_index * 2 * factor).astype(jnp.float32) / (2.0 * factor)
    local_index = lower_index - first_col
    columns = jnp.arange(width, dtype=jnp.int32)
    low_part = jnp.where(columns[None, :] == local_index[:, None], 1.0 - fraction[:, None], 0.0)
    high_part = jnp.where(columns[None, :] == local_index[:, None] + 1, fraction[:, None], 0.0)
    return low_part + high_part


def to_fine(field, counts, factor, plane_ids, line_ids, column_ids, first_z, first_y):
    width_z, width_y, width_x = field.shape
    along_z = interp_matrix(plane_ids, counts[0], factor, first_z, width_z)
    along_y = interp_matrix(line_ids, counts[1], factor, first_y, width_y)
    along_x = interp_matrix(column_ids, counts[2], factor, 0, width_x)
    section = jnp.einsum("fa,abc->fbc", along_z, field, precision=lax.Precision.HIGHEST)
    section = jnp.einsum("fb,abc->afc", along_y, section, precision=lax.Precision.HIGHEST)
    return jnp.einsum("fc,abc->abf", along_x, section, precision=lax.Precision.HIGHEST)


def top_coords(cell_ids, top_y, top_x):
    return (cell_ids // (top_y * top_x), cell_ids // top_x % top_y, cell_ids % top_x)


def top_potential(targets, charges_flat, top_z, top_y, top_x, strength):
    sources = jnp.arange(top_z * top_y * top_x, dtype=jnp.int32)
    target_xyz = top_coords(targets, top_y, top_x)
    source_xyz = top_coords(sources, top_y, top_x)
    distance = jnp.ones((targets.shape[0], sources.shape[0]), jnp.float32)
    for component in range(3):
        offset = (target_xyz[component][:, None] - source_xyz[component][None, :]).astype(
            jnp.float32
        )
        distance = distance + offset * offset
    kernel = strength / jnp.sqrt(distance)
    return jnp.dot(kernel, charges_flat, precision=lax.Precision.HIGHEST)


def gradient_along(padded, direction, plane_count, row_count, row_length):

    def shifted(offset_cells):
        corner = [2, 2, 2]
        corner[direction] = corner[direction] + offset_cells
        return padded[
            corner[0] : corner[0] + plane_count,
            corner[1] : corner[1] + row_count,
            corner[2] : corner[2] + row_length,
        ]

    return (8.0 * (shifted(1) - shifted(-1)) - (shifted(2) - shifted(-2))) / 12.0


def body(atom_cell, charge):
    slab_pos = lax.axis_index("slab")
    pencil_pos = lax.axis_index("pencil")
    slabs = lax.axis_size("slab")
    pencils = lax.axis_size("pencil")
    atom_total = charge.shape[0]
    row_cells = CZ * CY
    plane_row = (atom_cell[0] - slab_pos * CZ) * CY + (atom_cell[1] - pencil_pos * CY)
    column_of = atom_cell[2]
    block_atoms = math.gcd(atom_total, 512)
    block_count = atom_total // block_atoms
    row_blocks = plane_row.reshape(block_count, block_atoms)
    column_blocks = column_of.reshape(block_count, block_atoms)
    charge_blocks = charge.reshape(block_count, block_atoms)
    row_range = jnp.arange(row_cells, dtype=jnp.int32)
    column_range = jnp.arange(NX, dtype=jnp.int32)

    def deposit(total, block):
        rows_here, columns_here, charges_here = block
        row_table = (rows_here[:, None] == row_range[None, :]).astype(jnp.float32)
        column_table = jnp.where(
            columns_here[:, None] == column_range[None, :], charges_here[:, None], 0.0
        )
        added = jnp.dot(row_table.T, column_table, precision=lax.Precision.HIGHEST)
        return (total + added, None)

    charge_grid, _ = lax.scan(
        deposit, jnp.zeros((row_cells, NX), jnp.float32), (row_blocks, column_blocks, charge_blocks)
    )
    charge_grid = charge_grid.reshape(CZ, CY, NX)
    plane_ids = slab_pos * CZ + jnp.arange(CZ, dtype=jnp.int32)
    line_ids = pencil_pos * CY + jnp.arange(CY, dtype=jnp.int32)
    column_ids = jnp.arange(NX, dtype=jnp.int32)
    plane_level = CZ.bit_length() - 1
    rimmed = extended(charge_grid, (("slab", 0), ("pencil", 1)), RADIUS)
    padded = jnp.pad(rimmed, ((0, 0), (0, 0), (RADIUS, RADIUS)))
    potential = short_field(padded, CZ, CY, NX, RADIUS, kernel_weight)
    level_charge = charge_grid
    for level in range(1, plane_level):
        level_charge = restrict(level_charge)
        level_z, level_y, level_x = level_charge.shape
        cycle = extended(level_charge, (("slab", 0), ("pencil", 1)), RADIUS)
        cycle = jnp.pad(cycle, ((0, 0), (0, 0), (RADIUS, RADIUS)))
        field = short_field(
            cycle, level_z, level_y, level_x, RADIUS, partial(level_weight, 1.0 / 2**level)
        )
        framed = extended(field, (("slab", 0), ("pencil", 1)), 1)
        counts = (level_z * slabs, level_y * pencils, level_x)
        potential = potential + to_fine(
            framed,
            counts,
            2**level,
            plane_ids,
            line_ids,
            column_ids,
            slab_pos * level_z - 1,
            pencil_pos * level_y - 1,
        )
    own_plane = restrict(level_charge)[0]
    pieces = [own_plane]
    partial_plane = own_plane
    for level_bit in range(LEVELS - plane_level):
        partial_plane = restrict_plane(partial_plane)
        pieces.append(partial_plane)
    packed = jnp.concatenate([piece.reshape(1, -1) for piece in pieces], axis=1)
    gathered = lax.all_gather(packed, ("slab", "pencil"), axis=0, tiled=True)
    coarse = []
    offset = 0
    for step, piece in enumerate(pieces):
        rows, length = piece.shape
        group = 2**step
        block = gathered[:, offset : offset + rows * length].reshape(
            slabs // group, group, pencils, rows, length
        )
        grid = block.sum(axis=1)
        coarse.append(grid.reshape(slabs // group, pencils * rows, length))
        offset = offset + rows * length
    for step in range(LEVELS - plane_level):
        level = plane_level + step
        grid = coarse[step]
        level_z, level_y, level_x = grid.shape
        field = short_field(
            jnp.pad(grid, RADIUS),
            level_z,
            level_y,
            level_x,
            RADIUS,
            partial(level_weight, 1.0 / 2**level),
        )
        potential = potential + to_fine(
            field, field.shape, 2**level, plane_ids, line_ids, column_ids, 0, 0
        )
    top_grid = coarse[-1]
    top_z, top_y, top_x = top_grid.shape
    charges_flat = top_grid.reshape(top_z * top_y * top_x)
    top_total = top_z * top_y * top_x
    strength = 1.0 / F
    block_rows = math.gcd(top_total, 512)
    target_blocks = jnp.arange(top_total, dtype=jnp.int32).reshape(
        top_total // block_rows, block_rows
    )
    top_field = lax.map(
        lambda targets: top_potential(targets, charges_flat, top_z, top_y, top_x, strength),
        target_blocks,
    )
    top_field = top_field.reshape(top_z, top_y, top_x)
    potential = potential + to_fine(
        top_field, top_field.shape, F, plane_ids, line_ids, column_ids, 0, 0
    )
    rimmed_field = extended(potential, (("slab", 0), ("pencil", 1)), 2)
    padded_field = jnp.pad(rimmed_field, ((0, 0), (0, 0), (2, 2)))
    gradients = jnp.stack(
        [gradient_along(padded_field, direction, CZ, CY, NX) for direction in range(3)]
    ).reshape(3, row_cells, NX)

    def pick(block):
        rows_here, columns_here, charges_here = block
        row_table = (rows_here[:, None] == row_range[None, :]).astype(jnp.float32)
        column_table = (columns_here[:, None] == column_range[None, :]).astype(jnp.float32)
        picked_rows = jnp.einsum(
            "ar,drx->adx", row_table, gradients, precision=lax.Precision.HIGHEST
        )
        at_cell = jnp.sum(picked_rows * column_table[:, None, :], axis=2)
        return -charges_here[:, None] * at_cell

    picked = lax.map(pick, (row_blocks, column_blocks, charge_blocks))
    forces = picked.reshape(atom_total, 3).T
    return (potential, forces)


def solution(mesh):
    return jax.shard_map(
        body,
        mesh=mesh,
        in_specs=(P(None, ("slab", "pencil")), P(("slab", "pencil"))),
        out_specs=(P("slab", "pencil", None), P(None, ("slab", "pencil"))),
        check_vma=False,
    )
```

profile of v0, /device:TPU:12, one launch (start us, length us, event | category | flops | bytes accessed | tf_op | source)
XLA Modules:
  0.0 270.0 jit_solution(17136791525805690343)
XLA Ops:
  2.7 18.5 %while.27 = (s32[]{:T(128)}, f32[256,512]{1,0:T(8,128)S(1)}, s32[16,512]{1,0:T(8,128)S(1)}, s32[16,512]{1,0:T(8,128)S(1)}, f32[16,512]{1,0:T(8,128)S(1)}, /*index=5*/s32[]{:T(128)}, s32[]{:T(128)}) while((s32[]{:T(128)}, f32[256,512]{1,0:T(8,128)S(1)}, s32[16,512]{1,0:T(8,128)S(1)}, s32[16,512]{1,0:T(8,128)S(1)}, ...), condition=%wide.region_1.2_spmd.clone, body=%wide.region_0.1_spmd.clone.sunk | while | flops 806223872 | bytes 1067103 | solution.py:152
  21.2 34.9 %reshape_reshape.6 = f32[4,2,16,2,256,2]{5,4,3,2,1,0:T(8,128)} reshape(f32[256,512]{1,0:T(8,128)S(1)} %get-tuple-element.93) | data formatting | bytes 1048576 | tf_op jit(solution)/shard_map/reshape;reshape | solution.py:65
  56.1 11.6 %fusion.1208 = (f32[16,256]{1,0:T(8,128)S(1)}, f32[4,16,256]{2,1,0:T(8,128)S(1)}) fusion(f32[4,2,16,2,256,2]{5,4,3,2,1,0:T(8,128)} %reshape_reshape.6), kind=kLoop, calls=%fused_computation.2077 | loop fusion | flops 241664 | bytes 606208 | tf_op jit(solution)/shard_map/reduce_sum | solution.py:65
  67.7 5.5 %reshape.810 = f32[2,2,8,2,128,2]{5,4,3,2,1,0:T(8,128)} reshape(f32[4,16,256]{2,1,0:T(8,128)S(1)} %get-tuple-element.133) | data formatting | bytes 131072 | tf_op jit(solution)/shard_map/reshape | solution.py:65
  73.2 2.5 reduce_sum.100
  75.7 3.4 %collective-permute-start.12 = (f32[2,8,128]{2,1,0:T(8,128)S(1)}, f32[2,8,128]{2,1,0:T(8,128)S(1)}, u32[]{:S(2)}, u32[]{:S(2)}) collective-permute-start(f32[2,8,128]{2,1,0:T(8,128)S(1)} %reduce_sum.100), channel_id=1, source_target_pairs={{0,4},{4,8},{8,12},{12,16},{16,20},{20,24},{24,28},{1,5},{5,9},{9,... | collective-permute-start | bytes 24584 | tf_op jit(solution)/shard_map/ppermute | solution.py:24
  79.1 3.3 %collective-permute-start.13 = (f32[2,8,128]{2,1,0:T(8,128)S(1)}, f32[2,8,128]{2,1,0:T(8,128)S(1)}, u32[]{:S(2)}, u32[]{:S(2)}) collective-permute-start(f32[2,8,128]{2,1,0:T(8,128)S(1)} %reduce_sum.100), channel_id=1, source_target_pairs={{4,0},{8,4},{12,8},{16,12},{20,16},{24,20},{28,24},{5,1},{9,5},{13... | collective-permute-start | bytes 24584 | tf_op jit(solution)/shard_map/ppermute | solution.py:26
  85.1 4.2 %collective-permute-start.5 = (f32[2,16,256]{2,0,1:T(2,128)S(1)}, f32[2,16,256]{2,0,1:T(2,128)S(1)}, u32[]{:S(2)}, u32[]{:S(2)}) collective-permute-start(f32[2,16,256]{2,0,1:T(2,128)S(1)} %get-tuple-element.191), channel_id=1, source_target_pairs={{4,0},{8,4},{12,8},{16,12},{20,16},{24,20},{28,24},{5,1},{9,5},{13... | collective-permute-start | bytes 98312 | tf_op jit(solution)/shard_map/ppermute | solution.py:26
  95.0 30.5 %all-gather = f32[32,1,336]{2,1,0:T(1,128)S(1)} all-gather(f32[1,1,336]{2,1,0:T(1,128)S(1)} %maximum_bitcast_fusion), channel_id=1, replica_groups=mesh['slab'=8,'pencil'=4] {'slab','pencil'}, dimensions={0}, use_global_device_ids=true | all-gather | bytes 44352 | tf_op jit(solution)/shard_map/all_gather | solution.py:191
  133.4 4.5 %collective-permute-start.15 = (f32[6,2,128]{2,1,0:T(2,128)S(1)}, f32[6,2,128]{2,1,0:T(2,128)S(1)}, u32[]{:S(2)}, u32[]{:S(2)}) collective-permute-start(f32[6,2,128]{2,1,0:T(2,128)S(1)} %get-tuple-element.195), channel_id=1, source_target_pairs={{1,0},{2,1},{3,2},{5,4},{6,5},{7,6},{9,8},{10,9},{11,10},{13,12},{... | collective-permute-start | bytes 18440 | tf_op jit(solution)/shard_map/ppermute | solution.py:26
  141.5 6.0 %collective-permute-start.17 = (f32[1,8,128]{2,1,0:T(8,128)S(1)}, f32[1,8,128]{2,1,0:T(8,128)S(1)}, u32[]{:S(2)}, u32[]{:S(2)}) collective-permute-start(f32[1,8,128]{2,1,0:T(8,128)S(1)} %get-tuple-element.199), channel_id=1, source_target_pairs={{4,0},{8,4},{12,8},{16,12},{20,16},{24,20},{28,24},{5,1},{9,5},{13... | collective-permute-start | bytes 12296 | tf_op jit(solution)/shard_map/ppermute | solution.py:26
  147.6 5.4 %collective-permute-start.1 = (f32[2,32,512]{2,1,0:T(8,128)S(1)}, f32[2,32,512]{2,1,0:T(8,128)S(1)}, u32[]{:S(2)}, u32[]{:S(2)}) collective-permute-start(f32[2,32,512]{2,1,0:T(8,128)S(1)} %bitcast.128), channel_id=1, source_target_pairs={{4,0},{8,4},{12,8},{16,12},{20,16},{24,20},{28,24},{5,1},{9,5},{13... | collective-permute-start | bytes 393224 | tf_op jit(solution)/shard_map/ppermute | solution.py:26
  155.2 3.6 %collective-permute-start.19 = (f32[4,1,128]{2,1,0:T(1,128)S(1)}, f32[4,1,128]{2,1,0:T(1,128)S(1)}, u32[]{:S(2)}, u32[]{:S(2)}) collective-permute-start(f32[4,1,128]{2,1,0:T(1,128)S(1)} %get-tuple-element.197), channel_id=1, source_target_pairs={{1,0},{2,1},{3,2},{5,4},{6,5},{7,6},{9,8},{10,9},{11,10},{13,12},{... | collective-permute-start | bytes 6152 | tf_op jit(solution)/shard_map/ppermute | solution.py:26
  160.8 3.6 %collective-permute-start.7 = (f32[8,2,256]{2,0,1:T(8,128)S(1)}, f32[8,2,256]{2,0,1:T(8,128)S(1)}, u32[]{:S(2)}, u32[]{:S(2)}) collective-permute-start(f32[8,2,256]{2,0,1:T(8,128)S(1)} %get-tuple-element.185), channel_id=1, source_target_pairs={{1,0},{2,1},{3,2},{5,4},{6,5},{7,6},{9,8},{10,9},{11,10},{13,12},{... | collective-permute-start | bytes 49160 | tf_op jit(solution)/shard_map/ppermute | solution.py:26
  166.2 2.7 %fusion.468 = f32[4,16,256]{2,0,1:T(4,128)S(1)} fusion(f32[8,20,260]{2,0,1:T(8,128)S(1)} %select_maximum_fusion.8, f32[8,18,256]{2,0,1:T(8,128)S(1)} %get-tuple-element.183, f32[2,16,256]{2,0,1:T(2,128)S(1)} %collective-permute-done.5, f32[4,16,256]{2,0,1:T(4,128)S(1)} %copy.47, f32[8,18,256]{2,0,1:T(8,128)S(1)} %get-tuple-element.182, ...), kind=kLoop, calls=%fused_computation.912 | loop fusion | flops 4145152 | bytes 8060928 | tf_op jit(solution)/shard_map/add | solution.py:52
  170.9 4.8 %collective-permute-start.9 = (f32[1,16,256]{2,0,1:T(1,128)S(1)}, f32[1,16,256]{2,0,1:T(1,128)S(1)}, u32[]{:S(2)}, u32[]{:S(2)}) collective-permute-start(f32[1,16,256]{2,0,1:T(1,128)S(1)} %get-tuple-element.189), channel_id=1, source_target_pairs={{4,0},{8,4},{12,8},{16,12},{20,16},{24,20},{28,24},{5,1},{9,5},{13... | collective-permute-start | bytes 49160 | tf_op jit(solution)/shard_map/ppermute | solution.py:26
  179.1 3.6 %collective-permute-start.11 = (f32[6,1,256]{2,0,1:T(8,128)S(1)}, f32[6,1,256]{2,0,1:T(8,128)S(1)}, u32[]{:S(2)}, u32[]{:S(2)}) collective-permute-start(f32[6,1,256]{2,0,1:T(8,128)S(1)} %get-tuple-element.187), channel_id=1, source_target_pairs={{1,0},{2,1},{3,2},{5,4},{6,5},{7,6},{9,8},{10,9},{11,10},{13,12},{... | collective-permute-start | bytes 18440 | tf_op jit(solution)/shard_map/ppermute | solution.py:26
  186.4 3.6 %collective-permute-start.3 = (f32[12,2,512]{2,1,0:T(2,128)S(1)}, f32[12,2,512]{2,1,0:T(2,128)S(1)}, u32[]{:S(2)}, u32[]{:S(2)}) collective-permute-start(f32[12,2,512]{2,1,0:T(2,128)S(1)} %get-tuple-element.177), channel_id=1, source_target_pairs={{1,0},{2,1},{3,2},{5,4},{6,5},{7,6},{9,8},{10,9},{11,10},{13,12},{... | collective-permute-start | bytes 147464 | tf_op jit(solution)/shard_map/ppermute | solution.py:26
  192.5 10.7 %convolution_add_fusion.5 = f32[8,32,512]{2,1,0:T(8,128)S(1)} fusion(f32[8,32,256]{2,1,0:T(8,128)S(1)} %convolution_bitcast_fusion, f32[12,36,516]{2,1,0:T(8,128)S(1)} %select_maximum_fusion.4, f32[12,34,512]{2,1,0:T(8,128)S(1)} %get-tuple-element.175, f32[2,32,512]{2,1,0:T(8,128)S(1)} %collective-permute-done.1, f32[8,32,512]{2,1,0:T(8,128)S(1)} %bitcast.118, ...), kind=kOutput, calls=%fused_computation.282 | convolution fusion | flops 436600832 | bytes 64495616 | tf_op jit(solution)/shard_map/fc,abc->abf/dot_general | solution.py:91
  206.7 5.1 %collective-permute-start.20 = (f32[2,32,512]{2,1,0:T(8,128)S(1)}, f32[2,32,512]{2,1,0:T(8,128)S(1)}, u32[]{:S(2)}, u32[]{:S(2)}) collective-permute-start(f32[2,32,512]{2,1,0:T(8,128)S(1)} %get-tuple-element.179), channel_id=1, source_target_pairs={{4,0},{8,4},{12,8},{16,12},{20,16},{24,20},{28,24},{5,1},{9,5},{13... | collective-permute-start | bytes 393224 | tf_op jit(solution)/shard_map/ppermute | solution.py:26
  214.3 5.3 %collective-permute-done.21 = f32[2,32,512]{2,1,0:T(8,128)S(1)} collective-permute-done((f32[2,32,512]{2,1,0:T(8,128)S(1)}, f32[2,32,512]{2,1,0:T(8,128)S(1)}, u32[]{:S(2)}, u32[]{:S(2)}) %collective-permute-start.21) | collective-permute-done | bytes 131104 | tf_op jit(solution)/shard_map/ppermute | solution.py:24
  219.6 2.6 collective-permute-start.22
  224.5 3.1 %collective-permute-done.23 = f32[12,2,512]{2,1,0:T(2,128)S(1)} collective-permute-done((f32[12,2,512]{2,1,0:T(2,128)S(1)}, f32[12,2,512]{2,1,0:T(2,128)S(1)}, u32[]{:S(2)}, u32[]{:S(2)}) %collective-permute-start.23) | collective-permute-done | bytes 49184 | tf_op jit(solution)/shard_map/ppermute | solution.py:24
  229.6 40.4 %while.26 = (s32[]{:T(128)}, f32[16,512,3]{1,2,0:T(4,128)}, f32[16,512]{1,0:T(8,128)S(1)}, s32[16,512]{1,0:T(8,128)S(1)}, f32[3,256,512]{1,2,0:T(8,128)S(1)}, /*index=5*/s32[16,512]{1,0:T(8,128)S(1)}, s32[]{:T(128)}) while((s32[]{:T(128)}, f32[16,512,3]{1,2,0:T(4,128)}, f32[16,512]{1,0:T(8,128)S(1)}, s32[16,512]{1,0:T(8,128)S(1)}, ...), condition=%wide.region_18.19_spmd.clone, body=%wide.region_16.18_spmd.clone.sunk | while | flops 2418147840 | bytes 3709525 | solution.py:251
  (278 shorter events, 106.5 us)
Async XLA Ops:
  75.7 55.4 %collective-permute-start.12 = (f32[2,8,128]{2,1,0:T(8,128)S(1)}, f32[2,8,128]{2,1,0:T(8,128)S(1)}, u32[]{:S(2)}, u32[]{:S(2)}) collective-permute-start(f32[2,8,128]{2,1,0:T(8,128)S(1)} %reduce_sum.100), channel_id=1, source_target_pairs={{0,4},{4,8},{8,12},{12,16},{16,20},{20,24},{24,28},{1,5},{5,9},{9,... | collective-permute-start | bytes 24584 | tf_op jit(solution)/shard_map/ppermute | solution.py:24
  79.1 52.0 %collective-permute-start.13 = (f32[2,8,128]{2,1,0:T(8,128)S(1)}, f32[2,8,128]{2,1,0:T(8,128)S(1)}, u32[]{:S(2)}, u32[]{:S(2)}) collective-permute-start(f32[2,8,128]{2,1,0:T(8,128)S(1)} %reduce_sum.100), channel_id=1, source_target_pairs={{4,0},{8,4},{12,8},{16,12},{20,16},{24,20},{28,24},{5,1},{9,5},{13... | collective-permute-start | bytes 24584 | tf_op jit(solution)/shard_map/ppermute | solution.py:26
  82.5 72.6 %collective-permute-start.4 = (f32[2,16,256]{2,0,1:T(2,128)S(1)}, f32[2,16,256]{2,0,1:T(2,128)S(1)}, u32[]{:S(2)}, u32[]{:S(2)}) collective-permute-start(f32[2,16,256]{2,0,1:T(2,128)S(1)} %get-tuple-element.190), channel_id=1, source_target_pairs={{0,4},{4,8},{8,12},{12,16},{16,20},{20,24},{24,28},{1,5},{5,9},{9,... | collective-permute-start | bytes 98312 | tf_op jit(solution)/shard_map/ppermute | solution.py:24
  85.1 73.8 %collective-permute-start.5 = (f32[2,16,256]{2,0,1:T(2,128)S(1)}, f32[2,16,256]{2,0,1:T(2,128)S(1)}, u32[]{:S(2)}, u32[]{:S(2)}) collective-permute-start(f32[2,16,256]{2,0,1:T(2,128)S(1)} %get-tuple-element.191), channel_id=1, source_target_pairs={{4,0},{8,4},{12,8},{16,12},{20,16},{24,20},{28,24},{5,1},{9,5},{13... | collective-permute-start | bytes 98312 | tf_op jit(solution)/shard_map/ppermute | solution.py:26
  89.3 95.1 %collective-permute-start = (f32[2,32,512]{2,1,0:T(8,128)S(1)}, f32[2,32,512]{2,1,0:T(8,128)S(1)}, u32[]{:S(2)}, u32[]{:S(2)}) collective-permute-start(f32[2,32,512]{2,1,0:T(8,128)S(1)} %bitcast.129), channel_id=1, source_target_pairs={{0,4},{4,8},{8,12},{12,16},{16,20},{20,24},{24,28},{1,5},{5,9},{9,... | collective-permute-start | bytes 393224 | tf_op jit(solution)/shard_map/ppermute | solution.py:24
  131.1 6.8 %collective-permute-start.14 = (f32[6,2,128]{2,1,0:T(2,128)S(1)}, f32[6,2,128]{2,1,0:T(2,128)S(1)}, u32[]{:S(2)}, u32[]{:S(2)}) collective-permute-start(f32[6,2,128]{2,1,0:T(2,128)S(1)} %get-tuple-element.194), channel_id=1, source_target_pairs={{0,1},{1,2},{2,3},{4,5},{5,6},{6,7},{8,9},{9,10},{10,11},{12,13},{... | collective-permute-start | bytes 18440 | tf_op jit(solution)/shard_map/ppermute | solution.py:24
  133.4 5.8 %collective-permute-start.15 = (f32[6,2,128]{2,1,0:T(2,128)S(1)}, f32[6,2,128]{2,1,0:T(2,128)S(1)}, u32[]{:S(2)}, u32[]{:S(2)}) collective-permute-start(f32[6,2,128]{2,1,0:T(2,128)S(1)} %get-tuple-element.195), channel_id=1, source_target_pairs={{1,0},{2,1},{3,2},{5,4},{6,5},{7,6},{9,8},{10,9},{11,10},{13,12},{... | collective-permute-start | bytes 18440 | tf_op jit(solution)/shard_map/ppermute | solution.py:26
  139.6 8.0 %collective-permute-start.16 = (f32[1,8,128]{2,1,0:T(8,128)S(1)}, f32[1,8,128]{2,1,0:T(8,128)S(1)}, u32[]{:S(2)}, u32[]{:S(2)}) collective-permute-start(f32[1,8,128]{2,1,0:T(8,128)S(1)} %get-tuple-element.198), channel_id=1, source_target_pairs={{0,4},{4,8},{8,12},{12,16},{16,20},{20,24},{24,28},{1,5},{5,9},{9,... | collective-permute-start | bytes 12296 | tf_op jit(solution)/shard_map/ppermute | solution.py:24
  141.5 11.5 %collective-permute-start.17 = (f32[1,8,128]{2,1,0:T(8,128)S(1)}, f32[1,8,128]{2,1,0:T(8,128)S(1)}, u32[]{:S(2)}, u32[]{:S(2)}) collective-permute-start(f32[1,8,128]{2,1,0:T(8,128)S(1)} %get-tuple-element.199), channel_id=1, source_target_pairs={{4,0},{8,4},{12,8},{16,12},{20,16},{24,20},{28,24},{5,1},{9,5},{13... | collective-permute-start | bytes 12296 | tf_op jit(solution)/shard_map/ppermute | solution.py:26
  147.6 36.8 %collective-permute-start.1 = (f32[2,32,512]{2,1,0:T(8,128)S(1)}, f32[2,32,512]{2,1,0:T(8,128)S(1)}, u32[]{:S(2)}, u32[]{:S(2)}) collective-permute-start(f32[2,32,512]{2,1,0:T(8,128)S(1)} %bitcast.128), channel_id=1, source_target_pairs={{4,0},{8,4},{12,8},{16,12},{20,16},{24,20},{28,24},{5,1},{9,5},{13... | collective-permute-start | bytes 393224 | tf_op jit(solution)/shard_map/ppermute | solution.py:26
  153.1 7.7 %collective-permute-start.18 = (f32[4,1,128]{2,1,0:T(1,128)S(1)}, f32[4,1,128]{2,1,0:T(1,128)S(1)}, u32[]{:S(2)}, u32[]{:S(2)}) collective-permute-start(f32[4,1,128]{2,1,0:T(1,128)S(1)} %get-tuple-element.196), channel_id=1, source_target_pairs={{0,1},{1,2},{2,3},{4,5},{5,6},{6,7},{8,9},{9,10},{10,11},{12,13},{... | collective-permute-start | bytes 6152 | tf_op jit(solution)/shard_map/ppermute | solution.py:24
  155.2 9.3 %collective-permute-start.19 = (f32[4,1,128]{2,1,0:T(1,128)S(1)}, f32[4,1,128]{2,1,0:T(1,128)S(1)}, u32[]{:S(2)}, u32[]{:S(2)}) collective-permute-start(f32[4,1,128]{2,1,0:T(1,128)S(1)} %get-tuple-element.197), channel_id=1, source_target_pairs={{1,0},{2,1},{3,2},{5,4},{6,5},{7,6},{9,8},{10,9},{11,10},{13,12},{... | collective-permute-start | bytes 6152 | tf_op jit(solution)/shard_map/ppermute | solution.py:26
  158.9 5.6 %collective-permute-start.6 = (f32[8,2,256]{2,0,1:T(8,128)S(1)}, f32[8,2,256]{2,0,1:T(8,128)S(1)}, u32[]{:S(2)}, u32[]{:S(2)}) collective-permute-start(f32[8,2,256]{2,0,1:T(8,128)S(1)} %get-tuple-element.184), channel_id=1, source_target_pairs={{0,1},{1,2},{2,3},{4,5},{5,6},{6,7},{8,9},{9,10},{10,11},{12,13},{... | collective-permute-start | bytes 49160 | tf_op jit(solution)/shard_map/ppermute | solution.py:24
  160.8 5.1 %collective-permute-start.7 = (f32[8,2,256]{2,0,1:T(8,128)S(1)}, f32[8,2,256]{2,0,1:T(8,128)S(1)}, u32[]{:S(2)}, u32[]{:S(2)}) collective-permute-start(f32[8,2,256]{2,0,1:T(8,128)S(1)} %get-tuple-element.185), channel_id=1, source_target_pairs={{1,0},{2,1},{3,2},{5,4},{6,5},{7,6},{9,8},{10,9},{11,10},{13,12},{... | collective-permute-start | bytes 49160 | tf_op jit(solution)/shard_map/ppermute | solution.py:26
  169.0 7.0 %collective-permute-start.8 = (f32[1,16,256]{2,0,1:T(1,128)S(1)}, f32[1,16,256]{2,0,1:T(1,128)S(1)}, u32[]{:S(2)}, u32[]{:S(2)}) collective-permute-start(f32[1,16,256]{2,0,1:T(1,128)S(1)} %get-tuple-element.188), channel_id=1, source_target_pairs={{0,4},{4,8},{8,12},{12,16},{16,20},{20,24},{24,28},{1,5},{5,9},{9,... | collective-permute-start | bytes 49160 | tf_op jit(solution)/shard_map/ppermute | solution.py:24
  170.9 6.3 %collective-permute-start.9 = (f32[1,16,256]{2,0,1:T(1,128)S(1)}, f32[1,16,256]{2,0,1:T(1,128)S(1)}, u32[]{:S(2)}, u32[]{:S(2)}) collective-permute-start(f32[1,16,256]{2,0,1:T(1,128)S(1)} %get-tuple-element.189), channel_id=1, source_target_pairs={{4,0},{8,4},{12,8},{16,12},{20,16},{24,20},{28,24},{5,1},{9,5},{13... | collective-permute-start | bytes 49160 | tf_op jit(solution)/shard_map/ppermute | solution.py:26
  177.2 5.9 %collective-permute-start.10 = (f32[6,1,256]{2,0,1:T(8,128)S(1)}, f32[6,1,256]{2,0,1:T(8,128)S(1)}, u32[]{:S(2)}, u32[]{:S(2)}) collective-permute-start(f32[6,1,256]{2,0,1:T(8,128)S(1)} %get-tuple-element.186), channel_id=1, source_target_pairs={{0,1},{1,2},{2,3},{4,5},{5,6},{6,7},{8,9},{9,10},{10,11},{12,13},{... | collective-permute-start | bytes 18440 | tf_op jit(solution)/shard_map/ppermute | solution.py:24
  179.1 5.0 %collective-permute-start.11 = (f32[6,1,256]{2,0,1:T(8,128)S(1)}, f32[6,1,256]{2,0,1:T(8,128)S(1)}, u32[]{:S(2)}, u32[]{:S(2)}) collective-permute-start(f32[6,1,256]{2,0,1:T(8,128)S(1)} %get-tuple-element.187), channel_id=1, source_target_pairs={{1,0},{2,1},{3,2},{5,4},{6,5},{7,6},{9,8},{10,9},{11,10},{13,12},{... | collective-permute-start | bytes 18440 | tf_op jit(solution)/shard_map/ppermute | solution.py:26
  184.5 6.0 %collective-permute-start.2 = (f32[12,2,512]{2,1,0:T(2,128)S(1)}, f32[12,2,512]{2,1,0:T(2,128)S(1)}, u32[]{:S(2)}, u32[]{:S(2)}) collective-permute-start(f32[12,2,512]{2,1,0:T(2,128)S(1)} %get-tuple-element.176), channel_id=1, source_target_pairs={{0,1},{1,2},{2,3},{4,5},{5,6},{6,7},{8,9},{9,10},{10,11},{12,13},{... | collective-permute-start | bytes 147464 | tf_op jit(solution)/shard_map/ppermute | solution.py:24
  186.4 5.4 %collective-permute-start.3 = (f32[12,2,512]{2,1,0:T(2,128)S(1)}, f32[12,2,512]{2,1,0:T(2,128)S(1)}, u32[]{:S(2)}, u32[]{:S(2)}) collective-permute-start(f32[12,2,512]{2,1,0:T(2,128)S(1)} %get-tuple-element.177), channel_id=1, source_target_pairs={{1,0},{2,1},{3,2},{5,4},{6,5},{7,6},{9,8},{10,9},{11,10},{13,12},{... | collective-permute-start | bytes 147464 | tf_op jit(solution)/shard_map/ppermute | solution.py:26
  206.7 7.6 %collective-permute-start.20 = (f32[2,32,512]{2,1,0:T(8,128)S(1)}, f32[2,32,512]{2,1,0:T(8,128)S(1)}, u32[]{:S(2)}, u32[]{:S(2)}) collective-permute-start(f32[2,32,512]{2,1,0:T(8,128)S(1)} %get-tuple-element.179), channel_id=1, source_target_pairs={{4,0},{8,4},{12,8},{16,12},{20,16},{24,20},{28,24},{5,1},{9,5},{13... | collective-permute-start | bytes 393224 | tf_op jit(solution)/shard_map/ppermute | solution.py:26
  211.8 7.8 %collective-permute-start.21 = (f32[2,32,512]{2,1,0:T(8,128)S(1)}, f32[2,32,512]{2,1,0:T(8,128)S(1)}, u32[]{:S(2)}, u32[]{:S(2)}) collective-permute-start(f32[2,32,512]{2,1,0:T(8,128)S(1)} %get-tuple-element.178), channel_id=1, source_target_pairs={{0,4},{4,8},{8,12},{12,16},{16,20},{20,24},{24,28},{1,5},{5,9},{9,... | collective-permute-start | bytes 393224 | tf_op jit(solution)/shard_map/ppermute | solution.py:24
  219.6 4.8 %collective-permute-start.22 = (f32[12,2,512]{2,1,0:T(2,128)S(1)}, f32[12,2,512]{2,1,0:T(2,128)S(1)}, u32[]{:S(2)}, u32[]{:S(2)}) collective-permute-start(f32[12,2,512]{2,1,0:T(2,128)S(1)} %get-tuple-element.173), channel_id=1, source_target_pairs={{1,0},{2,1},{3,2},{5,4},{6,5},{7,6},{9,8},{10,9},{11,10},{13,12},{... | collective-permute-start | bytes 147464 | tf_op jit(solution)/shard_map/ppermute | solution.py:26
  222.2 5.4 %collective-permute-start.23 = (f32[12,2,512]{2,1,0:T(2,128)S(1)}, f32[12,2,512]{2,1,0:T(2,128)S(1)}, u32[]{:S(2)}, u32[]{:S(2)}) collective-permute-start(f32[12,2,512]{2,1,0:T(2,128)S(1)} %get-tuple-element.172), channel_id=1, source_target_pairs={{0,1},{1,2},{2,3},{4,5},{5,6},{6,7},{8,9},{9,10},{10,11},{12,13},{... | collective-permute-start | bytes 147464 | tf_op jit(solution)/shard_map/ppermute | solution.py:24
  (1 other events, 21.6 us)
where the time goes:
time: 271 us; the launch traced here: 270 us
  starting transfers between devices  76.4 us (28%)
  matrix products  65.5 us (24%)
  local copies, waits for them, and re-layouts  44.9 us (17%)
  other arithmetic  35 us (13%)
  blocking collectives  30.5 us (11%)
  waiting for transfers between devices  15.1 us (6%)
    ppermute x12, starting transfers between devices, extended(): lax.ppermute(head, axis, [((i + 1) % count, i) for i in range(ends)])  50.6 us
    another operation x1, local copies, waits for them, and re-layouts, restrict(): grid.reshape(planes // 2, 2, rows // 2, 2, length // 2, 2)  34.9 us
    all_gather x1, blocking collectives, body(): gathered = lax.all_gather(packed, ('slab', 'pencil'), axis=0, tiled=True)  30.5 us
    dot_general x16, matrix products, pick(): jnp.einsum('ar,drx->adx', row_table, gradients, precision=lax.Precision.H...  27.9 us
    ppermute x12, starting transfers between devices, extended(): lax.ppermute(tail, axis, [(i, (i + 1) % count) for i in range(ends)])  25.7 us
    dot_general x16, matrix products, deposit(): added = jnp.dot(row_table.T, column_table, precision=lax.Precision.HIGHEST)  17.4 us
    reduce_sum x4, other arithmetic, restrict(): grid.reshape(planes // 2, 2, rows // 2, 2, length // 2, 2)  14.4 us
    dot_general x5, matrix products, to_fine(): jnp.einsum('fc,abc->abf', along_x, section, precision=lax.Precision.HIGHEST)  14.1 us
  transfers between devices with their start and end apart: 24, of which 8 were waited for; matrix products, arithmetic and copies ran while one was open for 5% of the time, Pallas kernels for 0%

commit v1 on v0

--- a/solution.py
+++ b/solution.py
@@ -188,7 +188,8 @@
         partial_plane = restrict_plane(partial_plane)
         pieces.append(partial_plane)
     packed = jnp.concatenate([piece.reshape(1, -1) for piece in pieces], axis=1)
-    gathered = lax.all_gather(packed, ("slab", "pencil"), axis=0, tiled=True)
+    sent = jnp.stack([packed] * lax.axis_size(("slab", "pencil")))
+    gathered = jnp.concatenate(lax.all_to_all(sent, ("slab", "pencil"), 0, 0), axis=0)
     coarse = []
     offset = 0
     for step, piece in enumerate(pieces):

time: 271 us -> 242 us (0.89)
  blocking collectives: 30.5 us -> 0 us
    all_gather x1 -> x0, blocking collectives: 30.5 us -> none  [body(): gathered = lax.all_gather(packed, ('slab', 'pencil'), axis=0, tiled=True)]
    ppermute x12, starting transfers between devices: 50.6 us -> 40.8 us  [extended(): lax.ppermute(head, axis, [((i + 1) % count, i) for i in range(ends)])]
    all_to_all x0 -> x1, starting transfers between devices: none -> 6.4 us  [body(): lax.all_to_all(sent, ('slab', 'pencil'), 0, 0)]
    ppermute x12, starting transfers between devices: 25.7 us -> 29 us  [extended(): lax.ppermute(tail, axis, [(i, (i + 1) % count) for i in range(ends)])]
    ppermute x12, waiting for transfers between devices: 6.72 us -> 9.87 us  [extended(): lax.ppermute(head, axis, [((i + 1) % count, i) for i in range(ends)])]
  transfers between devices with their start and end apart: 24 -> 25, of which waited for: 8 -> 8; matrix products, arithmetic and copies ran while one was open for 5% -> 6% of each run, Pallas kernels for 0% -> 0%
where the time goes in v1:
time: 242 us; the launch traced here: 241 us
  starting transfers between devices  76.2 us (31%)
  matrix products  63.2 us (26%)
  local copies, waits for them, and re-layouts  45.5 us (19%)
  other arithmetic  36.9 us (15%)
  waiting for transfers between devices  16.3 us (7%)
    ppermute x12, starting transfers between devices, extended(): lax.ppermute(head, axis, [((i + 1) % count, i) for i in range(ends)])  40.8 us
    another operation x1, local copies, waits for them, and re-layouts, restrict(): grid.reshape(planes // 2, 2, rows // 2, 2, length // 2, 2)  34.9 us
    ppermute x12, starting transfers between devices, extended(): lax.ppermute(tail, axis, [(i, (i + 1) % count) for i in range(ends)])  29 us
    dot_general x16, matrix products, pick(): jnp.einsum('ar,drx->adx', row_table, gradients, precision=lax.Precision.H...  27.9 us
    dot_general x16, matrix products, deposit(): added = jnp.dot(row_table.T, column_table, precision=lax.Precision.HIGHEST)  17.4 us
    reduce_sum x4, other arithmetic, restrict(): grid.reshape(planes // 2, 2, rows // 2, 2, length // 2, 2)  14.4 us
    dot_general x5, matrix products, to_fine(): jnp.einsum('fc,abc->abf', along_x, section, precision=lax.Precision.HIGHEST)  14.1 us
    ppermute x12, waiting for transfers between devices, extended(): lax.ppermute(head, axis, [((i + 1) % count, i) for i in range(ends)])  9.87 us
  transfers between devices with their start and end apart: 25, of which 8 were waited for; matrix products, arithmetic and copies ran while one was open for 6% of the time, Pallas kernels for 0%

profile of v1, /device:TPU:12, one launch (start us, length us, event | category | flops | bytes accessed | tf_op | source)
XLA Modules:
  0.0 240.7 jit_solution(6588911675702108927)
XLA Ops:
  2.7 18.5 %while.27 = (s32[]{:T(128)}, f32[256,512]{1,0:T(8,128)S(1)}, s32[16,512]{1,0:T(8,128)S(1)}, s32[16,512]{1,0:T(8,128)S(1)}, f32[16,512]{1,0:T(8,128)S(1)}, /*index=5*/s32[]{:T(128)}, s32[]{:T(128)}) while((s32[]{:T(128)}, f32[256,512]{1,0:T(8,128)S(1)}, s32[16,512]{1,0:T(8,128)S(1)}, s32[16,512]{1,0:T(8,128)S(1)}, ...), condition=%wide.region_1.2_spmd.clone, body=%wide.region_0.1_spmd.clone.sunk | while | flops 806223872 | bytes 1067103 | solution.py:152
  21.2 34.9 %reshape_reshape.6 = f32[4,2,16,2,256,2]{5,4,3,2,1,0:T(8,128)} reshape(f32[256,512]{1,0:T(8,128)S(1)} %get-tuple-element.93) | data formatting | bytes 1048576 | tf_op jit(solution)/shard_map/reshape;reshape | solution.py:65
  56.1 11.6 %fusion.1154 = (f32[16,256]{1,0:T(8,128)S(1)}, f32[4,16,256]{2,1,0:T(8,128)S(1)}) fusion(f32[4,2,16,2,256,2]{5,4,3,2,1,0:T(8,128)} %reshape_reshape.6), kind=kLoop, calls=%fused_computation.2039 | loop fusion | flops 241664 | bytes 606208 | tf_op jit(solution)/shard_map/reduce_sum | solution.py:65
  67.7 5.5 %reshape.816 = f32[2,2,8,2,128,2]{5,4,3,2,1,0:T(8,128)} reshape(f32[4,16,256]{2,1,0:T(8,128)S(1)} %get-tuple-element.133) | data formatting | bytes 131072 | tf_op jit(solution)/shard_map/reshape | solution.py:65
  75.7 3.4 %collective-permute-start.12 = (f32[2,8,128]{2,1,0:T(8,128)S(1)}, f32[2,8,128]{2,1,0:T(8,128)S(1)}, u32[]{:S(2)}, u32[]{:S(2)}) collective-permute-start(f32[2,8,128]{2,1,0:T(8,128)S(1)} %reduce_sum.100), channel_id=1, source_target_pairs={{0,4},{4,8},{8,12},{12,16},{16,20},{20,24},{24,28},{1,5},{5,9},{9,... | collective-permute-start | bytes 24584 | tf_op jit(solution)/shard_map/ppermute | solution.py:24
  79.1 3.3 %collective-permute-start.13 = (f32[2,8,128]{2,1,0:T(8,128)S(1)}, f32[2,8,128]{2,1,0:T(8,128)S(1)}, u32[]{:S(2)}, u32[]{:S(2)}) collective-permute-start(f32[2,8,128]{2,1,0:T(8,128)S(1)} %reduce_sum.100), channel_id=1, source_target_pairs={{4,0},{8,4},{12,8},{16,12},{20,16},{24,20},{28,24},{5,1},{9,5},{13... | collective-permute-start | bytes 24584 | tf_op jit(solution)/shard_map/ppermute | solution.py:26
  85.1 4.2 %collective-permute-start.5 = (f32[2,16,256]{2,0,1:T(2,128)S(1)}, f32[2,16,256]{2,0,1:T(2,128)S(1)}, u32[]{:S(2)}, u32[]{:S(2)}) collective-permute-start(f32[2,16,256]{2,0,1:T(2,128)S(1)} %get-tuple-element.191), channel_id=1, source_target_pairs={{4,0},{8,4},{12,8},{16,12},{20,16},{24,20},{28,24},{5,1},{9,5},{13... | collective-permute-start | bytes 98312 | tf_op jit(solution)/shard_map/ppermute | solution.py:26
  95.4 6.4 %all-to-all-start = ((f32[32,1,336]{2,1,0:T(1,128)}), f32[32,1,336]{2,1,0:T(1,128)S(1)}, u32[]{:S(2)}, u32[]{:S(2)}) async-start(f32[32,1,336]{2,1,0:T(1,128)} %stack.10), calls=%async_computation | async-start | bytes 98304 | tf_op jit(solution)/shard_map/all_to_all | solution.py:192
  104.5 3.5 %collective-permute-start.15 = (f32[6,2,128]{2,1,0:T(2,128)S(1)}, f32[6,2,128]{2,1,0:T(2,128)S(1)}, u32[]{:S(2)}, u32[]{:S(2)}) collective-permute-start(f32[6,2,128]{2,1,0:T(2,128)S(1)} %get-tuple-element.195), channel_id=1, source_target_pairs={{1,0},{2,1},{3,2},{5,4},{6,5},{7,6},{9,8},{10,9},{11,10},{13,12},{... | collective-permute-start | bytes 18440 | tf_op jit(solution)/shard_map/ppermute | solution.py:26
  109.8 3.4 %collective-permute-start.16 = (f32[1,8,128]{2,1,0:T(8,128)S(1)}, f32[1,8,128]{2,1,0:T(8,128)S(1)}, u32[]{:S(2)}, u32[]{:S(2)}) collective-permute-start(f32[1,8,128]{2,1,0:T(8,128)S(1)} %get-tuple-element.198), channel_id=1, source_target_pairs={{0,4},{4,8},{8,12},{12,16},{16,20},{20,24},{24,28},{1,5},{5,9},{9,... | collective-permute-start | bytes 12296 | tf_op jit(solution)/shard_map/ppermute | solution.py:24
  113.2 3.4 %collective-permute-start.17 = (f32[1,8,128]{2,1,0:T(8,128)S(1)}, f32[1,8,128]{2,1,0:T(8,128)S(1)}, u32[]{:S(2)}, u32[]{:S(2)}) collective-permute-start(f32[1,8,128]{2,1,0:T(8,128)S(1)} %get-tuple-element.199), channel_id=1, source_target_pairs={{4,0},{8,4},{12,8},{16,12},{20,16},{24,20},{28,24},{5,1},{9,5},{13... | collective-permute-start | bytes 12296 | tf_op jit(solution)/shard_map/ppermute | solution.py:26
  121.0 3.6 %collective-permute-start.19 = (f32[4,1,128]{2,1,0:T(1,128)S(1)}, f32[4,1,128]{2,1,0:T(1,128)S(1)}, u32[]{:S(2)}, u32[]{:S(2)}) collective-permute-start(f32[4,1,128]{2,1,0:T(1,128)S(1)} %get-tuple-element.197), channel_id=1, source_target_pairs={{1,0},{2,1},{3,2},{5,4},{6,5},{7,6},{9,8},{10,9},{11,10},{13,12},{... | collective-permute-start | bytes 6152 | tf_op jit(solution)/shard_map/ppermute | solution.py:26
  126.6 3.6 %collective-permute-start.7 = (f32[8,2,256]{2,0,1:T(8,128)S(1)}, f32[8,2,256]{2,0,1:T(8,128)S(1)}, u32[]{:S(2)}, u32[]{:S(2)}) collective-permute-start(f32[8,2,256]{2,0,1:T(8,128)S(1)} %get-tuple-element.185), channel_id=1, source_target_pairs={{1,0},{2,1},{3,2},{5,4},{6,5},{7,6},{9,8},{10,9},{11,10},{13,12},{... | collective-permute-start | bytes 49160 | tf_op jit(solution)/shard_map/ppermute | solution.py:26
  132.0 2.7 %fusion.468 = f32[4,16,256]{2,0,1:T(4,128)S(1)} fusion(f32[8,20,260]{2,0,1:T(8,128)S(1)} %select_maximum_fusion.8, f32[8,18,256]{2,0,1:T(8,128)S(1)} %get-tuple-element.183, f32[2,16,256]{2,0,1:T(2,128)S(1)} %collective-permute-done.5, f32[4,16,256]{2,0,1:T(4,128)S(1)} %copy.59, f32[8,18,256]{2,0,1:T(8,128)S(1)} %get-tuple-element.182, ...), kind=kLoop, calls=%fused_computation.912 | loop fusion | flops 4145152 | bytes 8060928 | tf_op jit(solution)/shard_map/add | solution.py:52
  134.8 3.9 %collective-permute-start.8 = (f32[1,16,256]{2,0,1:T(1,128)S(1)}, f32[1,16,256]{2,0,1:T(1,128)S(1)}, u32[]{:S(2)}, u32[]{:S(2)}) collective-permute-start(f32[1,16,256]{2,0,1:T(1,128)S(1)} %get-tuple-element.188), channel_id=1, source_target_pairs={{0,4},{4,8},{8,12},{12,16},{16,20},{20,24},{24,28},{1,5},{5,9},{9,... | collective-permute-start | bytes 49160 | tf_op jit(solution)/shard_map/ppermute | solution.py:24
  138.7 2.8 %collective-permute-start.9 = (f32[1,16,256]{2,0,1:T(1,128)S(1)}, f32[1,16,256]{2,0,1:T(1,128)S(1)}, u32[]{:S(2)}, u32[]{:S(2)}) collective-permute-start(f32[1,16,256]{2,0,1:T(1,128)S(1)} %get-tuple-element.189), channel_id=1, source_target_pairs={{4,0},{8,4},{12,8},{16,12},{20,16},{24,20},{28,24},{5,1},{9,5},{13... | collective-permute-start | bytes 49160 | tf_op jit(solution)/shard_map/ppermute | solution.py:26
  146.3 3.8 %collective-permute-start.11 = (f32[6,1,256]{2,0,1:T(8,128)S(1)}, f32[6,1,256]{2,0,1:T(8,128)S(1)}, u32[]{:S(2)}, u32[]{:S(2)}) collective-permute-start(f32[6,1,256]{2,0,1:T(8,128)S(1)} %get-tuple-element.187), channel_id=1, source_target_pairs={{1,0},{2,1},{3,2},{5,4},{6,5},{7,6},{9,8},{10,9},{11,10},{13,12},{... | collective-permute-start | bytes 18440 | tf_op jit(solution)/shard_map/ppermute | solution.py:26
  158.5 3.6 %collective-permute-start.3 = (f32[12,2,512]{2,1,0:T(2,128)S(1)}, f32[12,2,512]{2,1,0:T(2,128)S(1)}, u32[]{:S(2)}, u32[]{:S(2)}) collective-permute-start(f32[12,2,512]{2,1,0:T(2,128)S(1)} %get-tuple-element.177), channel_id=1, source_target_pairs={{1,0},{2,1},{3,2},{5,4},{6,5},{7,6},{9,8},{10,9},{11,10},{13,12},{... | collective-permute-start | bytes 147464 | tf_op jit(solution)/shard_map/ppermute | solution.py:26
  164.6 10.7 %convolution_add_fusion.5 = f32[8,32,512]{2,1,0:T(8,128)S(1)} fusion(f32[8,32,256]{2,1,0:T(8,128)S(1)} %convolution_bitcast_fusion, f32[12,36,516]{2,1,0:T(8,128)S(1)} %select_maximum_fusion.4, f32[12,34,512]{2,1,0:T(8,128)S(1)} %get-tuple-element.175, f32[2,32,512]{2,1,0:T(8,128)S(1)} %collective-permute-done.1, f32[8,32,512]{2,1,0:T(8,128)S(1)} %bitcast.116, ...), kind=kOutput, calls=%fused_computation.282 | convolution fusion | flops 436600832 | bytes 64495616 | tf_op jit(solution)/shard_map/fc,abc->abf/dot_general | solution.py:91
  178.8 3.7 %collective-permute-start.20 = (f32[2,32,512]{2,1,0:T(8,128)S(1)}, f32[2,32,512]{2,1,0:T(8,128)S(1)}, u32[]{:S(2)}, u32[]{:S(2)}) collective-permute-start(f32[2,32,512]{2,1,0:T(8,128)S(1)} %get-tuple-element.179), channel_id=1, source_target_pairs={{4,0},{8,4},{12,8},{16,12},{20,16},{24,20},{28,24},{5,1},{9,5},{13... | collective-permute-start | bytes 393224 | tf_op jit(solution)/shard_map/ppermute | solution.py:26
  187.0 3.2 %collective-permute-done.21 = f32[2,32,512]{2,1,0:T(8,128)S(1)} collective-permute-done((f32[2,32,512]{2,1,0:T(8,128)S(1)}, f32[2,32,512]{2,1,0:T(8,128)S(1)}, u32[]{:S(2)}, u32[]{:S(2)}) %collective-permute-start.21) | collective-permute-done | bytes 131104 | tf_op jit(solution)/shard_map/ppermute | solution.py:24
  190.3 2.6 %collective-permute-start.22 = (f32[12,2,512]{2,1,0:T(2,128)S(1)}, f32[12,2,512]{2,1,0:T(2,128)S(1)}, u32[]{:S(2)}, u32[]{:S(2)}) collective-permute-start(f32[12,2,512]{2,1,0:T(2,128)S(1)} %get-tuple-element.173), channel_id=1, source_target_pairs={{1,0},{2,1},{3,2},{5,4},{6,5},{7,6},{9,8},{10,9},{11,10},{13,12},{... | collective-permute-start | bytes 147464 | tf_op jit(solution)/shard_map/ppermute | solution.py:26
  195.2 3.1 %collective-permute-done.23 = f32[12,2,512]{2,1,0:T(2,128)S(1)} collective-permute-done((f32[12,2,512]{2,1,0:T(2,128)S(1)}, f32[12,2,512]{2,1,0:T(2,128)S(1)}, u32[]{:S(2)}, u32[]{:S(2)}) %collective-permute-start.23) | collective-permute-done | bytes 49184 | tf_op jit(solution)/shard_map/ppermute | solution.py:24
  200.3 40.4 %while.26 = (s32[]{:T(128)}, f32[16,512,3]{1,2,0:T(4,128)}, f32[16,512]{1,0:T(8,128)S(1)}, s32[16,512]{1,0:T(8,128)S(1)}, f32[3,256,512]{1,2,0:T(8,128)S(1)}, /*index=5*/s32[16,512]{1,0:T(8,128)S(1)}, s32[]{:T(128)}) while((s32[]{:T(128)}, f32[16,512,3]{1,2,0:T(4,128)}, f32[16,512]{1,0:T(8,128)S(1)}, s32[16,512]{1,0:T(8,128)S(1)}, ...), condition=%wide.region_18.19_spmd.clone, body=%wide.region_16.18_spmd.clone.sunk | while | flops 2418147840 | bytes 3709525 | solution.py:252
  (280 shorter events, 110.8 us)
Async XLA Ops:
  75.7 26.8 %collective-permute-start.12 = (f32[2,8,128]{2,1,0:T(8,128)S(1)}, f32[2,8,128]{2,1,0:T(8,128)S(1)}, u32[]{:S(2)}, u32[]{:S(2)}) collective-permute-start(f32[2,8,128]{2,1,0:T(8,128)S(1)} %reduce_sum.100), channel_id=1, source_target_pairs={{0,4},{4,8},{8,12},{12,16},{16,20},{20,24},{24,28},{1,5},{5,9},{9,... | collective-permute-start | bytes 24584 | tf_op jit(solution)/shard_map/ppermute | solution.py:24
  79.1 23.4 %collective-permute-start.13 = (f32[2,8,128]{2,1,0:T(8,128)S(1)}, f32[2,8,128]{2,1,0:T(8,128)S(1)}, u32[]{:S(2)}, u32[]{:S(2)}) collective-permute-start(f32[2,8,128]{2,1,0:T(8,128)S(1)} %reduce_sum.100), channel_id=1, source_target_pairs={{4,0},{8,4},{12,8},{16,12},{20,16},{24,20},{28,24},{5,1},{9,5},{13... | collective-permute-start | bytes 24584 | tf_op jit(solution)/shard_map/ppermute | solution.py:26
  82.6 38.4 %collective-permute-start.4 = (f32[2,16,256]{2,0,1:T(2,128)S(1)}, f32[2,16,256]{2,0,1:T(2,128)S(1)}, u32[]{:S(2)}, u32[]{:S(2)}) collective-permute-start(f32[2,16,256]{2,0,1:T(2,128)S(1)} %get-tuple-element.190), channel_id=1, source_target_pairs={{0,4},{4,8},{8,12},{12,16},{16,20},{20,24},{24,28},{1,5},{5,9},{9,... | collective-permute-start | bytes 98312 | tf_op jit(solution)/shard_map/ppermute | solution.py:24
  85.1 39.6 %collective-permute-start.5 = (f32[2,16,256]{2,0,1:T(2,128)S(1)}, f32[2,16,256]{2,0,1:T(2,128)S(1)}, u32[]{:S(2)}, u32[]{:S(2)}) collective-permute-start(f32[2,16,256]{2,0,1:T(2,128)S(1)} %get-tuple-element.191), channel_id=1, source_target_pairs={{4,0},{8,4},{12,8},{16,12},{20,16},{24,20},{28,24},{5,1},{9,5},{13... | collective-permute-start | bytes 98312 | tf_op jit(solution)/shard_map/ppermute | solution.py:26
  89.3 67.2 %collective-permute-start = (f32[2,32,512]{2,1,0:T(8,128)S(1)}, f32[2,32,512]{2,1,0:T(8,128)S(1)}, u32[]{:S(2)}, u32[]{:S(2)}) collective-permute-start(f32[2,32,512]{2,1,0:T(8,128)S(1)} %bitcast.127), channel_id=1, source_target_pairs={{0,4},{4,8},{8,12},{12,16},{16,20},{20,24},{24,28},{1,5},{5,9},{9,... | collective-permute-start | bytes 393224 | tf_op jit(solution)/shard_map/ppermute | solution.py:24
  95.4 56.7 %all-to-all-start = ((f32[32,1,336]{2,1,0:T(1,128)}), f32[32,1,336]{2,1,0:T(1,128)S(1)}, u32[]{:S(2)}, u32[]{:S(2)}) async-start(f32[32,1,336]{2,1,0:T(1,128)} %stack.10), calls=%async_computation | async-start | bytes 98304 | tf_op jit(solution)/shard_map/all_to_all | solution.py:192
  102.5 5.6 %collective-permute-start.14 = (f32[6,2,128]{2,1,0:T(2,128)S(1)}, f32[6,2,128]{2,1,0:T(2,128)S(1)}, u32[]{:S(2)}, u32[]{:S(2)}) collective-permute-start(f32[6,2,128]{2,1,0:T(2,128)S(1)} %get-tuple-element.194), channel_id=1, source_target_pairs={{0,1},{1,2},{2,3},{4,5},{5,6},{6,7},{8,9},{9,10},{10,11},{12,13},{... | collective-permute-start | bytes 18440 | tf_op jit(solution)/shard_map/ppermute | solution.py:24
  104.5 4.9 %collective-permute-start.15 = (f32[6,2,128]{2,1,0:T(2,128)S(1)}, f32[6,2,128]{2,1,0:T(2,128)S(1)}, u32[]{:S(2)}, u32[]{:S(2)}) collective-permute-start(f32[6,2,128]{2,1,0:T(2,128)S(1)} %get-tuple-element.195), channel_id=1, source_target_pairs={{1,0},{2,1},{3,2},{5,4},{6,5},{7,6},{9,8},{10,9},{11,10},{13,12},{... | collective-permute-start | bytes 18440 | tf_op jit(solution)/shard_map/ppermute | solution.py:26
  109.8 6.8 %collective-permute-start.16 = (f32[1,8,128]{2,1,0:T(8,128)S(1)}, f32[1,8,128]{2,1,0:T(8,128)S(1)}, u32[]{:S(2)}, u32[]{:S(2)}) collective-permute-start(f32[1,8,128]{2,1,0:T(8,128)S(1)} %get-tuple-element.198), channel_id=1, source_target_pairs={{0,4},{4,8},{8,12},{12,16},{16,20},{20,24},{24,28},{1,5},{5,9},{9,... | collective-permute-start | bytes 12296 | tf_op jit(solution)/shard_map/ppermute | solution.py:24
  113.2 5.9 %collective-permute-start.17 = (f32[1,8,128]{2,1,0:T(8,128)S(1)}, f32[1,8,128]{2,1,0:T(8,128)S(1)}, u32[]{:S(2)}, u32[]{:S(2)}) collective-permute-start(f32[1,8,128]{2,1,0:T(8,128)S(1)} %get-tuple-element.199), channel_id=1, source_target_pairs={{4,0},{8,4},{12,8},{16,12},{20,16},{24,20},{28,24},{5,1},{9,5},{13... | collective-permute-start | bytes 12296 | tf_op jit(solution)/shard_map/ppermute | solution.py:26
  116.6 39.9 %collective-permute-start.1 = (f32[2,32,512]{2,1,0:T(8,128)S(1)}, f32[2,32,512]{2,1,0:T(8,128)S(1)}, u32[]{:S(2)}, u32[]{:S(2)}) collective-permute-start(f32[2,32,512]{2,1,0:T(8,128)S(1)} %bitcast.126), channel_id=1, source_target_pairs={{4,0},{8,4},{12,8},{16,12},{20,16},{24,20},{28,24},{5,1},{9,5},{13... | collective-permute-start | bytes 393224 | tf_op jit(solution)/shard_map/ppermute | solution.py:26
  119.1 7.6 %collective-permute-start.18 = (f32[4,1,128]{2,1,0:T(1,128)S(1)}, f32[4,1,128]{2,1,0:T(1,128)S(1)}, u32[]{:S(2)}, u32[]{:S(2)}) collective-permute-start(f32[4,1,128]{2,1,0:T(1,128)S(1)} %get-tuple-element.196), channel_id=1, source_target_pairs={{0,1},{1,2},{2,3},{4,5},{5,6},{6,7},{8,9},{9,10},{10,11},{12,13},{... | collective-permute-start | bytes 6152 | tf_op jit(solution)/shard_map/ppermute | solution.py:24
  121.0 9.3 %collective-permute-start.19 = (f32[4,1,128]{2,1,0:T(1,128)S(1)}, f32[4,1,128]{2,1,0:T(1,128)S(1)}, u32[]{:S(2)}, u32[]{:S(2)}) collective-permute-start(f32[4,1,128]{2,1,0:T(1,128)S(1)} %get-tuple-element.197), channel_id=1, source_target_pairs={{1,0},{2,1},{3,2},{5,4},{6,5},{7,6},{9,8},{10,9},{11,10},{13,12},{... | collective-permute-start | bytes 6152 | tf_op jit(solution)/shard_map/ppermute | solution.py:26
  124.7 5.6 %collective-permute-start.6 = (f32[8,2,256]{2,0,1:T(8,128)S(1)}, f32[8,2,256]{2,0,1:T(8,128)S(1)}, u32[]{:S(2)}, u32[]{:S(2)}) collective-permute-start(f32[8,2,256]{2,0,1:T(8,128)S(1)} %get-tuple-element.184), channel_id=1, source_target_pairs={{0,1},{1,2},{2,3},{4,5},{5,6},{6,7},{8,9},{9,10},{10,11},{12,13},{... | collective-permute-start | bytes 49160 | tf_op jit(solution)/shard_map/ppermute | solution.py:24
  126.6 5.1 %collective-permute-start.7 = (f32[8,2,256]{2,0,1:T(8,128)S(1)}, f32[8,2,256]{2,0,1:T(8,128)S(1)}, u32[]{:S(2)}, u32[]{:S(2)}) collective-permute-start(f32[8,2,256]{2,0,1:T(8,128)S(1)} %get-tuple-element.185), channel_id=1, source_target_pairs={{1,0},{2,1},{3,2},{5,4},{6,5},{7,6},{9,8},{10,9},{11,10},{13,12},{... | collective-permute-start | bytes 49160 | tf_op jit(solution)/shard_map/ppermute | solution.py:26
  134.8 7.0 %collective-permute-start.8 = (f32[1,16,256]{2,0,1:T(1,128)S(1)}, f32[1,16,256]{2,0,1:T(1,128)S(1)}, u32[]{:S(2)}, u32[]{:S(2)}) collective-permute-start(f32[1,16,256]{2,0,1:T(1,128)S(1)} %get-tuple-element.188), channel_id=1, source_target_pairs={{0,4},{4,8},{8,12},{12,16},{16,20},{20,24},{24,28},{1,5},{5,9},{9,... | collective-permute-start | bytes 49160 | tf_op jit(solution)/shard_map/ppermute | solution.py:24
  138.7 5.6 %collective-permute-start.9 = (f32[1,16,256]{2,0,1:T(1,128)S(1)}, f32[1,16,256]{2,0,1:T(1,128)S(1)}, u32[]{:S(2)}, u32[]{:S(2)}) collective-permute-start(f32[1,16,256]{2,0,1:T(1,128)S(1)} %get-tuple-element.189), channel_id=1, source_target_pairs={{4,0},{8,4},{12,8},{16,12},{20,16},{24,20},{28,24},{5,1},{9,5},{13... | collective-permute-start | bytes 49160 | tf_op jit(solution)/shard_map/ppermute | solution.py:26
  144.4 6.1 %collective-permute-start.10 = (f32[6,1,256]{2,0,1:T(8,128)S(1)}, f32[6,1,256]{2,0,1:T(8,128)S(1)}, u32[]{:S(2)}, u32[]{:S(2)}) collective-permute-start(f32[6,1,256]{2,0,1:T(8,128)S(1)} %get-tuple-element.186), channel_id=1, source_target_pairs={{0,1},{1,2},{2,3},{4,5},{5,6},{6,7},{8,9},{9,10},{10,11},{12,13},{... | collective-permute-start | bytes 18440 | tf_op jit(solution)/shard_map/ppermute | solution.py:24
  146.3 5.0 %collective-permute-start.11 = (f32[6,1,256]{2,0,1:T(8,128)S(1)}, f32[6,1,256]{2,0,1:T(8,128)S(1)}, u32[]{:S(2)}, u32[]{:S(2)}) collective-permute-start(f32[6,1,256]{2,0,1:T(8,128)S(1)} %get-tuple-element.187), channel_id=1, source_target_pairs={{1,0},{2,1},{3,2},{5,4},{6,5},{7,6},{9,8},{10,9},{11,10},{13,12},{... | collective-permute-start | bytes 18440 | tf_op jit(solution)/shard_map/ppermute | solution.py:26
  156.6 5.9 %collective-permute-start.2 = (f32[12,2,512]{2,1,0:T(2,128)S(1)}, f32[12,2,512]{2,1,0:T(2,128)S(1)}, u32[]{:S(2)}, u32[]{:S(2)}) collective-permute-start(f32[12,2,512]{2,1,0:T(2,128)S(1)} %get-tuple-element.176), channel_id=1, source_target_pairs={{0,1},{1,2},{2,3},{4,5},{5,6},{6,7},{8,9},{9,10},{10,11},{12,13},{... | collective-permute-start | bytes 147464 | tf_op jit(solution)/shard_map/ppermute | solution.py:24
  158.5 5.4 %collective-permute-start.3 = (f32[12,2,512]{2,1,0:T(2,128)S(1)}, f32[12,2,512]{2,1,0:T(2,128)S(1)}, u32[]{:S(2)}, u32[]{:S(2)}) collective-permute-start(f32[12,2,512]{2,1,0:T(2,128)S(1)} %get-tuple-element.177), channel_id=1, source_target_pairs={{1,0},{2,1},{3,2},{5,4},{6,5},{7,6},{9,8},{10,9},{11,10},{13,12},{... | collective-permute-start | bytes 147464 | tf_op jit(solution)/shard_map/ppermute | solution.py:26
  178.8 8.3 %collective-permute-start.20 = (f32[2,32,512]{2,1,0:T(8,128)S(1)}, f32[2,32,512]{2,1,0:T(8,128)S(1)}, u32[]{:S(2)}, u32[]{:S(2)}) collective-permute-start(f32[2,32,512]{2,1,0:T(8,128)S(1)} %get-tuple-element.179), channel_id=1, source_target_pairs={{4,0},{8,4},{12,8},{16,12},{20,16},{24,20},{28,24},{5,1},{9,5},{13... | collective-permute-start | bytes 393224 | tf_op jit(solution)/shard_map/ppermute | solution.py:26
  182.5 7.8 %collective-permute-start.21 = (f32[2,32,512]{2,1,0:T(8,128)S(1)}, f32[2,32,512]{2,1,0:T(8,128)S(1)}, u32[]{:S(2)}, u32[]{:S(2)}) collective-permute-start(f32[2,32,512]{2,1,0:T(8,128)S(1)} %get-tuple-element.178), channel_id=1, source_target_pairs={{0,4},{4,8},{8,12},{12,16},{16,20},{20,24},{24,28},{1,5},{5,9},{9,... | collective-permute-start | bytes 393224 | tf_op jit(solution)/shard_map/ppermute | solution.py:24
  192.9 5.4 %collective-permute-start.23 = (f32[12,2,512]{2,1,0:T(2,128)S(1)}, f32[12,2,512]{2,1,0:T(2,128)S(1)}, u32[]{:S(2)}, u32[]{:S(2)}) collective-permute-start(f32[12,2,512]{2,1,0:T(2,128)S(1)} %get-tuple-element.172), channel_id=1, source_target_pairs={{0,1},{1,2},{2,3},{4,5},{5,6},{6,7},{8,9},{9,10},{10,11},{12,13},{... | collective-permute-start | bytes 147464 | tf_op jit(solution)/shard_map/ppermute | solution.py:24
  (2 other events, 25.0 us)
